TPU v7x, 512 devices: a whole 4x4x16 slice. The times are simulated.
512 devices in a mesh: grid: 32 (over x, y, core), band: 16 (over z).
Axes of the slice: x: 4, y: 4, z: 16, core: 2. Of those that a mesh axis runs over, the one named last changes fastest.
Arguments:
- orbitals: bfloat16 [32768, 512], P('grid', 'band'), may hold values from -6 to 6
- rotation: bfloat16 [512, 32768], P('grid', 'band'), may hold values from -0.25 to 0.25
Outputs:
- rotated: bfloat16 [32768, 32768], P('grid', 'band')
All inputs are finite; a program needn't handle non-finite values.
Results may differ from a plain program's by a relative error of at most 0.001.
Values may be sent and summed in bfloat16 or wider, within the bound.
No kernel may reach another device: no remote copies, remote signals or barrier semaphores. Data moves between devices by JAX's collectives and lax.ppermute only.
A program may use at most 64 MiB of HBM per device.

v0:
```python
import jax
import jax.numpy as jnp
from jax import lax
from jax.sharding import PartitionSpec as P


def on_device(orbitals, rotation):
    all_cols = lax.all_gather(orbitals, "band", axis=1, tiled=True)
    all_rows = lax.all_gather(rotation, "grid", axis=0, tiled=True)
    total = jnp.dot(all_cols, all_rows, preferred_element_type=jnp.float32)
    return total.astype(jnp.bfloat16)


def solution(mesh):
    in_specs = (P("grid", "band"), P("grid", "band"))
    out_specs = P("grid", "band")
    return jax.shard_map(
        on_device, mesh=mesh, in_specs=in_specs, out_specs=out_specs, check_vma=False
    )
```

profile of v0, /device:TPU:1, one launch (start us, length us, event | category | flops | bytes accessed | tf_op | source)
XLA Modules:
  0.0 158.6 jit_solution(7569212816232975436)
XLA Ops:
  6.5 0.0 all-gather.3.cloned.1.call-start
  6.5 0.7 all-gather.3.cloned.1.call-update
  7.3 0.0 all-gather.5.cloned.1.call-start
  7.3 0.7 all-gather.5.cloned.1.call-update
  8.0 68.3 %all-gather.3.cloned.1.call-done = bf16[1024,512]{0,1:T(8,128)(2,1)} async-done(((bf16[1024,32]{0,1:T(8,128)(2,1)}), bf16[1024,512]{0,1:T(8,128)(2,1)}) %all-gather.3.cloned.1.call-update) | async-done | bytes 1048592 | tf_op jit(solution)/shard_map/all_gather | solution.py:8
  76.3 69.1 %all-gather.5.cloned.1.call-done = bf16[512,2048]{1,0:T(8,128)(2,1)} async-done(((bf16[16,2048]{1,0:T(8,128)(2,1)}), bf16[512,2048]{1,0:T(8,128)(2,1)}) %all-gather.5.cloned.1.call-update) | async-done | bytes 2097168 | tf_op jit(solution)/shard_map/all_gather | solution.py:9
  145.4 6.3 %convolution_convert_fusion = bf16[1024,2048]{1,0:T(8,128)(2,1)} fusion(bf16[1024,512]{0,1:T(8,128)(2,1)} %all-gather.3.cloned.1.call-done, bf16[512,2048]{1,0:T(8,128)(2,1)} %all-gather.5.cloned.1.call-done), kind=kOutput, calls=%fused_computation | convolution fusion | flops 2149580800 | bytes 7340032 | tf_op jit(solution)/shard_map/dot_general | solution.py:10
Async XLA Ops:
  6.5 69.8 %all-gather.3.cloned.1.call-start = ((), (), s32[]{:S(2)}) async-start(), calls=%async_computation | async-start | bytes 1114112 | tf_op jit(solution)/shard_map/all_gather | solution.py:8
  7.3 138.2 %all-gather.5.cloned.1.call-start = ((), (), s32[]{:S(2)}) async-start(), calls=%async_computation.1 | async-start | bytes 2162688 | tf_op jit(solution)/shard_map/all_gather | solution.py:9
Sparse Core Ops, SparseCore 0:
  9.4 66.8 all-gather.2
  79.5 65.8 all-gather.4
where the time goes:
time: 159 us
  waiting for transfers between devices  139 us (87%)
  between operations  13.4 us (8%)
  matrix products  6.32 us (4%)
    all_gather x1, waiting for transfers between devices, on_device(): all_rows = lax.all_gather(rotation, 'grid', axis=0, tiled=True)  69.1 us
    all_gather x1, waiting for transfers between devices, on_device(): all_cols = lax.all_gather(orbitals, 'band', axis=1, tiled=True)  68.3 us
    dot_general x1, matrix products, on_device(): total = jnp.dot(all_cols, all_rows, preferred_element_type=jnp.float32)  6.32 us
  transfers between devices with their start and end apart: 2, of which 2 were waited for; matrix products, arithmetic and copies ran while one was open for 0% of the time, Pallas kernels for 0%

commit v1 on v0

--- a/solution.py
+++ b/solution.py
@@ -5,7 +5,12 @@
 
 
 def on_device(orbitals, rotation):
-    all_cols = lax.all_gather(orbitals, "band", axis=1, tiled=True)
+    ring = [orbitals]
+    for hop in range(15):
+        ring.append(lax.ppermute(ring[-1], "band", [(dev, (dev + 1) % 16) for dev in range(16)]))
+    all_cols = jnp.roll(
+        jnp.concatenate(ring[::-1], axis=1), (lax.axis_index("band") + 1) * ring[0].shape[1], axis=1
+    )
     all_rows = lax.all_gather(rotation, "grid", axis=0, tiled=True)
     total = jnp.dot(all_cols, all_rows, preferred_element_type=jnp.float32)
     return total.astype(jnp.bfloat16)

time: 159 us -> 147 us (0.925)
  waiting for transfers between devices: 139 us -> 95.2 us
  starting transfers between devices: 0.04 us -> 31.2 us
    ppermute x0 -> x15, waiting for transfers between devices: none -> 71.5 us  [on_device(): lax.ppermute(ring[-1], 'band', [(dev, (dev + 1) % 16) for dev in range(16)])]
    all_gather x1 -> x0, waiting for transfers between devices: 68.3 us -> none  [on_device(): all_cols = lax.all_gather(orbitals, 'band', axis=1, tiled=True)]
    all_gather x1, waiting for transfers between devices: 69.1 us -> 23.7 us  [on_device(): all_rows = lax.all_gather(rotation, 'grid', axis=0, tiled=True)]
    ppermute x0 -> x15, starting transfers between devices: none -> 31.2 us  [on_device(): lax.ppermute(ring[-1], 'band', [(dev, (dev + 1) % 16) for dev in range(16)])]
  transfers between devices with their start and end apart: 2 -> 16, of which waited for: 2 -> 16; matrix products, arithmetic and copies ran while one was open for 0% -> 0% of each run, Pallas kernels for 0% -> 0%
where the time goes in v1:
time: 147 us; the launch traced here: 146 us
  waiting for transfers between devices  95.2 us (65%)
  starting transfers between devices  31.2 us (21%)
  between operations  13.8 us (9%)
  matrix products  5.99 us (4%)
    ppermute x15, waiting for transfers between devices, on_device(): lax.ppermute(ring[-1], 'band', [(dev, (dev + 1) % 16) for dev in range(16)])  71.5 us
    ppermute x15, starting transfers between devices, on_device(): lax.ppermute(ring[-1], 'band', [(dev, (dev + 1) % 16) for dev in range(16)])  31.2 us
    all_gather x1, waiting for transfers between devices, on_device(): all_rows = lax.all_gather(rotation, 'grid', axis=0, tiled=True)  23.7 us
    dot_general x1, matrix products, on_device(): total = jnp.dot(all_cols, all_rows, preferred_element_type=jnp.float32)  5.99 us
  transfers between devices with their start and end apart: 16, of which 16 were waited for; matrix products, arithmetic and copies ran while one was open for 0% of the time, Pallas kernels for 0%

profile of v1, /device:TPU:1, one launch (start us, length us, event | category | flops | bytes accessed | tf_op | source)
XLA Modules:
  0.0 146.4 jit_solution(11834522624852118642)
XLA Ops:
  6.5 4.5 %collective-permute-start = (bf16[1024,32]{0,1:T(8,128)(2,1)}, bf16[1024,32]{0,1:T(8,128)(2,1)S(1)}, u32[]{:S(2)}, u32[]{:S(2)}) collective-permute-start(bf16[1024,32]{0,1:T(8,128)(2,1)} %param.2), channel_id=1, source_target_pairs={{0,1},{1,2},{2,3},{3,4},{4,5},{5,6},{6,7},{7,8},{8,9},{9,10},{10,1... | collective-permute-start | bytes 196616 | tf_op jit(solution)/shard_map/ppermute | solution.py:10
  11.0 9.4 %collective-permute-done = bf16[1024,32]{0,1:T(8,128)(2,1)S(1)} collective-permute-done((bf16[1024,32]{0,1:T(8,128)(2,1)}, bf16[1024,32]{0,1:T(8,128)(2,1)S(1)}, u32[]{:S(2)}, u32[]{:S(2)}) %collective-permute-start) | collective-permute-done | bytes 65568 | tf_op jit(solution)/shard_map/ppermute | solution.py:10
  20.5 1.9 %collective-permute-start.1 = (bf16[1024,32]{0,1:T(8,128)(2,1)S(1)}, bf16[1024,32]{0,1:T(8,128)(2,1)S(1)}, u32[]{:S(2)}, u32[]{:S(2)}) collective-permute-start(bf16[1024,32]{0,1:T(8,128)(2,1)S(1)} %collective-permute-done), channel_id=1, source_target_pairs={{0,1},{1,2},{2,3},{3,4},{4,5},{5,6},{6,7},{7,8},{8,9},{9,10},{10,1... | collective-permute-start | bytes 196616 | tf_op jit(solution)/shard_map/ppermute | solution.py:10
  22.4 4.3 %collective-permute-done.1 = bf16[1024,32]{0,1:T(8,128)(2,1)S(1)} collective-permute-done((bf16[1024,32]{0,1:T(8,128)(2,1)S(1)}, bf16[1024,32]{0,1:T(8,128)(2,1)S(1)}, u32[]{:S(2)}, u32[]{:S(2)}) %collective-permute-start.1) | collective-permute-done | bytes 65568 | tf_op jit(solution)/shard_map/ppermute | solution.py:10
  26.7 1.9 %collective-permute-start.2 = (bf16[1024,32]{0,1:T(8,128)(2,1)S(1)}, bf16[1024,32]{0,1:T(8,128)(2,1)S(1)}, u32[]{:S(2)}, u32[]{:S(2)}) collective-permute-start(bf16[1024,32]{0,1:T(8,128)(2,1)S(1)} %collective-permute-done.1), channel_id=1, source_target_pairs={{0,1},{1,2},{2,3},{3,4},{4,5},{5,6},{6,7},{7,8},{8,9},{9,10},{10,1... | collective-permute-start | bytes 196616 | tf_op jit(solution)/shard_map/ppermute | solution.py:10
  28.6 4.3 %collective-permute-done.2 = bf16[1024,32]{0,1:T(8,128)(2,1)S(1)} collective-permute-done((bf16[1024,32]{0,1:T(8,128)(2,1)S(1)}, bf16[1024,32]{0,1:T(8,128)(2,1)S(1)}, u32[]{:S(2)}, u32[]{:S(2)}) %collective-permute-start.2) | collective-permute-done | bytes 65568 | tf_op jit(solution)/shard_map/ppermute | solution.py:10
  32.9 1.9 %collective-permute-start.3 = (bf16[1024,32]{0,1:T(8,128)(2,1)S(1)}, bf16[1024,32]{0,1:T(8,128)(2,1)S(1)}, u32[]{:S(2)}, u32[]{:S(2)}) collective-permute-start(bf16[1024,32]{0,1:T(8,128)(2,1)S(1)} %collective-permute-done.2), channel_id=1, source_target_pairs={{0,1},{1,2},{2,3},{3,4},{4,5},{5,6},{6,7},{7,8},{8,9},{9,10},{10,1... | collective-permute-start | bytes 196616 | tf_op jit(solution)/shard_map/ppermute | solution.py:10
  34.8 4.3 %collective-permute-done.3 = bf16[1024,32]{0,1:T(8,128)(2,1)S(1)} collective-permute-done((bf16[1024,32]{0,1:T(8,128)(2,1)S(1)}, bf16[1024,32]{0,1:T(8,128)(2,1)S(1)}, u32[]{:S(2)}, u32[]{:S(2)}) %collective-permute-start.3) | collective-permute-done | bytes 65568 | tf_op jit(solution)/shard_map/ppermute | solution.py:10
  39.1 1.9 %collective-permute-start.4 = (bf16[1024,32]{0,1:T(8,128)(2,1)S(1)}, bf16[1024,32]{0,1:T(8,128)(2,1)S(1)}, u32[]{:S(2)}, u32[]{:S(2)}) collective-permute-start(bf16[1024,32]{0,1:T(8,128)(2,1)S(1)} %collective-permute-done.3), channel_id=1, source_target_pairs={{0,1},{1,2},{2,3},{3,4},{4,5},{5,6},{6,7},{7,8},{8,9},{9,10},{10,1... | collective-permute-start | bytes 196616 | tf_op jit(solution)/shard_map/ppermute | solution.py:10
  41.0 4.3 %collective-permute-done.4 = bf16[1024,32]{0,1:T(8,128)(2,1)S(1)} collective-permute-done((bf16[1024,32]{0,1:T(8,128)(2,1)S(1)}, bf16[1024,32]{0,1:T(8,128)(2,1)S(1)}, u32[]{:S(2)}, u32[]{:S(2)}) %collective-permute-start.4) | collective-permute-done | bytes 65568 | tf_op jit(solution)/shard_map/ppermute | solution.py:10
  47.2 4.3 %collective-permute-done.5 = bf16[1024,32]{0,1:T(8,128)(2,1)S(1)} collective-permute-done((bf16[1024,32]{0,1:T(8,128)(2,1)S(1)}, bf16[1024,32]{0,1:T(8,128)(2,1)S(1)}, u32[]{:S(2)}, u32[]{:S(2)}) %collective-permute-start.5) | collective-permute-done | bytes 65568 | tf_op jit(solution)/shard_map/ppermute | solution.py:10
  53.4 5.0 %collective-permute-done.6 = bf16[1024,32]{0,1:T(8,128)(2,1)S(1)} collective-permute-done((bf16[1024,32]{0,1:T(8,128)(2,1)S(1)}, bf16[1024,32]{0,1:T(8,128)(2,1)S(1)}, u32[]{:S(2)}, u32[]{:S(2)}) %collective-permute-start.6) | collective-permute-done | bytes 65568 | tf_op jit(solution)/shard_map/ppermute | solution.py:10
  58.4 1.9 %collective-permute-start.7 = (bf16[1024,32]{0,1:T(8,128)(2,1)S(1)}, bf16[1024,32]{0,1:T(8,128)(2,1)S(1)}, u32[]{:S(2)}, u32[]{:S(2)}) collective-permute-start(bf16[1024,32]{0,1:T(8,128)(2,1)S(1)} %collective-permute-done.6), channel_id=1, source_target_pairs={{0,1},{1,2},{2,3},{3,4},{4,5},{5,6},{6,7},{7,8},{8,9},{9,10},{10,1... | collective-permute-start | bytes 196616 | tf_op jit(solution)/shard_map/ppermute | solution.py:10
  60.3 4.3 %collective-permute-done.7 = bf16[1024,32]{0,1:T(8,128)(2,1)S(1)} collective-permute-done((bf16[1024,32]{0,1:T(8,128)(2,1)S(1)}, bf16[1024,32]{0,1:T(8,128)(2,1)S(1)}, u32[]{:S(2)}, u32[]{:S(2)}) %collective-permute-start.7) | collective-permute-done | bytes 65568 | tf_op jit(solution)/shard_map/ppermute | solution.py:10
  66.6 4.3 %collective-permute-done.8 = bf16[1024,32]{0,1:T(8,128)(2,1)S(1)} collective-permute-done((bf16[1024,32]{0,1:T(8,128)(2,1)S(1)}, bf16[1024,32]{0,1:T(8,128)(2,1)S(1)}, u32[]{:S(2)}, u32[]{:S(2)}) %collective-permute-start.8) | collective-permute-done | bytes 65568 | tf_op jit(solution)/shard_map/ppermute | solution.py:10
  72.8 4.3 %collective-permute-done.9 = bf16[1024,32]{0,1:T(8,128)(2,1)S(1)} collective-permute-done((bf16[1024,32]{0,1:T(8,128)(2,1)S(1)}, bf16[1024,32]{0,1:T(8,128)(2,1)S(1)}, u32[]{:S(2)}, u32[]{:S(2)}) %collective-permute-start.9) | collective-permute-done | bytes 65568 | tf_op jit(solution)/shard_map/ppermute | solution.py:10
  77.0 1.9 %collective-permute-start.10 = (bf16[1024,32]{0,1:T(8,128)(2,1)S(1)}, bf16[1024,32]{0,1:T(8,128)(2,1)S(1)}, u32[]{:S(2)}, u32[]{:S(2)}) collective-permute-start(bf16[1024,32]{0,1:T(8,128)(2,1)S(1)} %collective-permute-done.9), channel_id=1, source_target_pairs={{0,1},{1,2},{2,3},{3,4},{4,5},{5,6},{6,7},{7,8},{8,9},{9,10},{10,1... | collective-permute-start | bytes 196616 | tf_op jit(solution)/shard_map/ppermute | solution.py:10
  79.0 4.3 %collective-permute-done.10 = bf16[1024,32]{0,1:T(8,128)(2,1)S(1)} collective-permute-done((bf16[1024,32]{0,1:T(8,128)(2,1)S(1)}, bf16[1024,32]{0,1:T(8,128)(2,1)S(1)}, u32[]{:S(2)}, u32[]{:S(2)}) %collective-permute-start.10) | collective-permute-done | bytes 65568 | tf_op jit(solution)/shard_map/ppermute | solution.py:10
  85.2 4.3 %collective-permute-done.11 = bf16[1024,32]{0,1:T(8,128)(2,1)S(1)} collective-permute-done((bf16[1024,32]{0,1:T(8,128)(2,1)S(1)}, bf16[1024,32]{0,1:T(8,128)(2,1)S(1)}, u32[]{:S(2)}, u32[]{:S(2)}) %collective-permute-start.11) | collective-permute-done | bytes 65568 | tf_op jit(solution)/shard_map/ppermute | solution.py:10
  91.4 4.9 %collective-permute-done.12 = bf16[1024,32]{0,1:T(8,128)(2,1)S(1)} collective-permute-done((bf16[1024,32]{0,1:T(8,128)(2,1)S(1)}, bf16[1024,32]{0,1:T(8,128)(2,1)S(1)}, u32[]{:S(2)}, u32[]{:S(2)}) %collective-permute-start.12) | collective-permute-done | bytes 65568 | tf_op jit(solution)/shard_map/ppermute | solution.py:10
  98.2 5.0 %collective-permute-done.13 = bf16[1024,32]{0,1:T(8,128)(2,1)S(1)} collective-permute-done((bf16[1024,32]{0,1:T(8,128)(2,1)S(1)}, bf16[1024,32]{0,1:T(8,128)(2,1)S(1)}, u32[]{:S(2)}, u32[]{:S(2)}) %collective-permute-start.13) | collective-permute-done | bytes 65568 | tf_op jit(solution)/shard_map/ppermute | solution.py:10
  105.2 4.3 %collective-permute-done.14 = bf16[1024,32]{0,1:T(8,128)(2,1)S(1)} collective-permute-done((bf16[1024,32]{0,1:T(8,128)(2,1)S(1)}, bf16[1024,32]{0,1:T(8,128)(2,1)S(1)}, u32[]{:S(2)}, u32[]{:S(2)}) %collective-permute-start.14) | collective-permute-done | bytes 65568 | tf_op jit(solution)/shard_map/ppermute | solution.py:10
  109.9 23.7 %all-gather.2.cloned.1.call-done = bf16[512,2048]{1,0:T(8,128)(2,1)} async-done(((bf16[16,2048]{1,0:T(8,128)(2,1)}), bf16[512,2048]{1,0:T(8,128)(2,1)}) %all-gather.2.cloned.1.call-update) | async-done | bytes 2097168 | tf_op jit(solution)/shard_map/all_gather | solution.py:14
  133.6 6.0 %convolution_convert_fusion = bf16[1024,2048]{1,0:T(8,128)(2,1)} fusion(bf16[512,2048]{1,0:T(8,128)(2,1)} %all-gather.2.cloned.1.call-done, bf16[1024,1024]{0,1:T(8,128)(2,1)S(1)} %constant_dynamic-update-slice_fusion, s32[]{:T(128)S(6)} %select_n.14), kind=kOutput, calls=%fused_computation | convolution fusion | flops 2149580800 | bytes 7340036 | tf_op jit(solution)/shard_map/dot_general | solution.py:15
  (44 shorter events, 15.5 us)
Async XLA Ops:
  6.5 103.1 %copy-start = (bf16[1024,32]{0,1:T(8,128)(2,1)S(1)}, bf16[1024,32]{0,1:T(8,128)(2,1)}, u32[]{:S(2)}) copy-start(bf16[1024,32]{0,1:T(8,128)(2,1)} %param.2) | copy-start | bytes 196612
  6.5 127.0 %all-gather.2.cloned.1.call-start = ((), (), s32[]{:S(2)}) async-start(), calls=%async_computation | async-start | bytes 2162688 | tf_op jit(solution)/shard_map/all_gather | solution.py:14
  6.5 13.9 %collective-permute-start = (bf16[1024,32]{0,1:T(8,128)(2,1)}, bf16[1024,32]{0,1:T(8,128)(2,1)S(1)}, u32[]{:S(2)}, u32[]{:S(2)}) collective-permute-start(bf16[1024,32]{0,1:T(8,128)(2,1)} %param.2), channel_id=1, source_target_pairs={{0,1},{1,2},{2,3},{3,4},{4,5},{5,6},{6,7},{7,8},{8,9},{9,10},{10,1... | collective-permute-start | bytes 196616 | tf_op jit(solution)/shard_map/ppermute | solution.py:10
  20.5 6.2 %collective-permute-start.1 = (bf16[1024,32]{0,1:T(8,128)(2,1)S(1)}, bf16[1024,32]{0,1:T(8,128)(2,1)S(1)}, u32[]{:S(2)}, u32[]{:S(2)}) collective-permute-start(bf16[1024,32]{0,1:T(8,128)(2,1)S(1)} %collective-permute-done), channel_id=1, source_target_pairs={{0,1},{1,2},{2,3},{3,4},{4,5},{5,6},{6,7},{7,8},{8,9},{9,10},{10,1... | collective-permute-start | bytes 196616 | tf_op jit(solution)/shard_map/ppermute | solution.py:10
  26.7 6.2 %collective-permute-start.2 = (bf16[1024,32]{0,1:T(8,128)(2,1)S(1)}, bf16[1024,32]{0,1:T(8,128)(2,1)S(1)}, u32[]{:S(2)}, u32[]{:S(2)}) collective-permute-start(bf16[1024,32]{0,1:T(8,128)(2,1)S(1)} %collective-permute-done.1), channel_id=1, source_target_pairs={{0,1},{1,2},{2,3},{3,4},{4,5},{5,6},{6,7},{7,8},{8,9},{9,10},{10,1... | collective-permute-start | bytes 196616 | tf_op jit(solution)/shard_map/ppermute | solution.py:10
  32.9 6.2 %collective-permute-start.3 = (bf16[1024,32]{0,1:T(8,128)(2,1)S(1)}, bf16[1024,32]{0,1:T(8,128)(2,1)S(1)}, u32[]{:S(2)}, u32[]{:S(2)}) collective-permute-start(bf16[1024,32]{0,1:T(8,128)(2,1)S(1)} %collective-permute-done.2), channel_id=1, source_target_pairs={{0,1},{1,2},{2,3},{3,4},{4,5},{5,6},{6,7},{7,8},{8,9},{9,10},{10,1... | collective-permute-start | bytes 196616 | tf_op jit(solution)/shard_map/ppermute | solution.py:10
  39.1 6.2 %collective-permute-start.4 = (bf16[1024,32]{0,1:T(8,128)(2,1)S(1)}, bf16[1024,32]{0,1:T(8,128)(2,1)S(1)}, u32[]{:S(2)}, u32[]{:S(2)}) collective-permute-start(bf16[1024,32]{0,1:T(8,128)(2,1)S(1)} %collective-permute-done.3), channel_id=1, source_target_pairs={{0,1},{1,2},{2,3},{3,4},{4,5},{5,6},{6,7},{7,8},{8,9},{9,10},{10,1... | collective-permute-start | bytes 196616 | tf_op jit(solution)/shard_map/ppermute | solution.py:10
  45.3 6.2 %collective-permute-start.5 = (bf16[1024,32]{0,1:T(8,128)(2,1)S(1)}, bf16[1024,32]{0,1:T(8,128)(2,1)S(1)}, u32[]{:S(2)}, u32[]{:S(2)}) collective-permute-start(bf16[1024,32]{0,1:T(8,128)(2,1)S(1)} %collective-permute-done.4), channel_id=1, source_target_pairs={{0,1},{1,2},{2,3},{3,4},{4,5},{5,6},{6,7},{7,8},{8,9},{9,10},{10,1... | collective-permute-start | bytes 196616 | tf_op jit(solution)/shard_map/ppermute | solution.py:10
  51.5 6.9 %collective-permute-start.6 = (bf16[1024,32]{0,1:T(8,128)(2,1)S(1)}, bf16[1024,32]{0,1:T(8,128)(2,1)S(1)}, u32[]{:S(2)}, u32[]{:S(2)}) collective-permute-start(bf16[1024,32]{0,1:T(8,128)(2,1)S(1)} %collective-permute-done.5), channel_id=1, source_target_pairs={{0,1},{1,2},{2,3},{3,4},{4,5},{5,6},{6,7},{7,8},{8,9},{9,10},{10,1... | collective-permute-start | bytes 196616 | tf_op jit(solution)/shard_map/ppermute | solution.py:10
  58.4 6.2 %collective-permute-start.7 = (bf16[1024,32]{0,1:T(8,128)(2,1)S(1)}, bf16[1024,32]{0,1:T(8,128)(2,1)S(1)}, u32[]{:S(2)}, u32[]{:S(2)}) collective-permute-start(bf16[1024,32]{0,1:T(8,128)(2,1)S(1)} %collective-permute-done.6), channel_id=1, source_target_pairs={{0,1},{1,2},{2,3},{3,4},{4,5},{5,6},{6,7},{7,8},{8,9},{9,10},{10,1... | collective-permute-start | bytes 196616 | tf_op jit(solution)/shard_map/ppermute | solution.py:10
  64.6 6.2 %collective-permute-start.8 = (bf16[1024,32]{0,1:T(8,128)(2,1)S(1)}, bf16[1024,32]{0,1:T(8,128)(2,1)S(1)}, u32[]{:S(2)}, u32[]{:S(2)}) collective-permute-start(bf16[1024,32]{0,1:T(8,128)(2,1)S(1)} %collective-permute-done.7), channel_id=1, source_target_pairs={{0,1},{1,2},{2,3},{3,4},{4,5},{5,6},{6,7},{7,8},{8,9},{9,10},{10,1... | collective-permute-start | bytes 196616 | tf_op jit(solution)/shard_map/ppermute | solution.py:10
  70.8 6.2 %collective-permute-start.9 = (bf16[1024,32]{0,1:T(8,128)(2,1)S(1)}, bf16[1024,32]{0,1:T(8,128)(2,1)S(1)}, u32[]{:S(2)}, u32[]{:S(2)}) collective-permute-start(bf16[1024,32]{0,1:T(8,128)(2,1)S(1)} %collective-permute-done.8), channel_id=1, source_target_pairs={{0,1},{1,2},{2,3},{3,4},{4,5},{5,6},{6,7},{7,8},{8,9},{9,10},{10,1... | collective-permute-start | bytes 196616 | tf_op jit(solution)/shard_map/ppermute | solution.py:10
  77.0 6.2 %collective-permute-start.10 = (bf16[1024,32]{0,1:T(8,128)(2,1)S(1)}, bf16[1024,32]{0,1:T(8,128)(2,1)S(1)}, u32[]{:S(2)}, u32[]{:S(2)}) collective-permute-start(bf16[1024,32]{0,1:T(8,128)(2,1)S(1)} %collective-permute-done.9), channel_id=1, source_target_pairs={{0,1},{1,2},{2,3},{3,4},{4,5},{5,6},{6,7},{7,8},{8,9},{9,10},{10,1... | collective-permute-start | bytes 196616 | tf_op jit(solution)/shard_map/ppermute | solution.py:10
  83.3 6.2 %collective-permute-start.11 = (bf16[1024,32]{0,1:T(8,128)(2,1)S(1)}, bf16[1024,32]{0,1:T(8,128)(2,1)S(1)}, u32[]{:S(2)}, u32[]{:S(2)}) collective-permute-start(bf16[1024,32]{0,1:T(8,128)(2,1)S(1)} %collective-permute-done.10), channel_id=1, source_target_pairs={{0,1},{1,2},{2,3},{3,4},{4,5},{5,6},{6,7},{7,8},{8,9},{9,10},{10,1... | collective-permute-start | bytes 196616 | tf_op jit(solution)/shard_map/ppermute | solution.py:10
  89.5 6.9 %collective-permute-start.12 = (bf16[1024,32]{0,1:T(8,128)(2,1)S(1)}, bf16[1024,32]{0,1:T(8,128)(2,1)S(1)}, u32[]{:S(2)}, u32[]{:S(2)}) collective-permute-start(bf16[1024,32]{0,1:T(8,128)(2,1)S(1)} %collective-permute-done.11), channel_id=1, source_target_pairs={{0,1},{1,2},{2,3},{3,4},{4,5},{5,6},{6,7},{7,8},{8,9},{9,10},{10,1... | collective-permute-start | bytes 196616 | tf_op jit(solution)/shard_map/ppermute | solution.py:10
  96.3 6.9 %collective-permute-start.13 = (bf16[1024,32]{0,1:T(8,128)(2,1)S(1)}, bf16[1024,32]{0,1:T(8,128)(2,1)S(1)}, u32[]{:S(2)}, u32[]{:S(2)}) collective-permute-start(bf16[1024,32]{0,1:T(8,128)(2,1)S(1)} %collective-permute-done.12), channel_id=1, source_target_pairs={{0,1},{1,2},{2,3},{3,4},{4,5},{5,6},{6,7},{7,8},{8,9},{9,10},{10,1... | collective-permute-start | bytes 196616 | tf_op jit(solution)/shard_map/ppermute | solution.py:10
  103.2 6.2 %collective-permute-start.14 = (bf16[1024,32]{0,1:T(8,128)(2,1)S(1)}, bf16[1024,32]{0,1:T(8,128)(2,1)S(1)}, u32[]{:S(2)}, u32[]{:S(2)}) collective-permute-start(bf16[1024,32]{0,1:T(8,128)(2,1)S(1)} %collective-permute-done.13), channel_id=1, source_target_pairs={{0,1},{1,2},{2,3},{3,4},{4,5},{5,6},{6,7},{7,8},{8,9},{9,10},{10,1... | collective-permute-start | bytes 196616 | tf_op jit(solution)/shard_map/ppermute | solution.py:10
Sparse Core Ops, SparseCore 0:
  66.7 66.8 all-gather.1
